TPU v7x, 256 devices: a whole 4x4x8 slice. The times are simulated.
256 devices in a mesh: cohort: 4 (over x), dev: 64 (over z, y, core).
Axes of the slice: x: 4, y: 4, z: 8, core: 2. Of those that a mesh axis runs over, the one named last changes fastest.
Arguments:
- dosage: bfloat16 [524288, 2048], P(('cohort', 'dev')), may hold values from 0 to 2
- allele_freq: float32 [2048], replicated, may hold values from 0.05 to 0.5
- probes: bfloat16 [2048, 512], replicated, may hold values from -6 to 6
- owner_perm: int32 [2048], replicated, may hold values from 0 to 2047, each once
Outputs:
- projected: float32 [2048, 512], P('dev')
Inputs may be any that keep to these rules, and one draw needn't show every extreme that they name: `owner_perm`: each SNP appears exactly once.
All inputs are finite; a program needn't handle non-finite values.
Results may differ from a plain program's by a relative error of at most 0.00044.
Values sent between devices are 32-bit elements; how exact they have to be, the bound alone decides.
No kernel may reach another device: no remote copies, remote signals or barrier semaphores. Data moves between devices by JAX's collectives and lax.ppermute only.
A program may use at most 128 MiB of HBM per device.

v0:
```python
import functools

import jax
import jax.numpy as jnp
from jax import lax
from jax.experimental import pallas as pl
from jax.experimental.pallas import tpu as pltpu
from jax.sharding import Mesh, PartitionSpec as P


NX, NZ, NY, NC = 4, 8, 4, 2
B = 128
NB = 4
G8 = 8
PAIRS = [(i, j) for i in range(NB) for j in range(i, NB)]
HALF = len(PAIRS) // 2
ROWS = HALF * B // (NX * NY)

TN = (((0,), (0,)), ((), ()))


def dot(a, b, dims):
    return lax.dot_general(a, b, dims, preferred_element_type=jnp.float32)


def centre(d_ref, f_ref):
    freq = f_ref[...]
    scale = 1.0 / jnp.sqrt(2.0 * freq * (1.0 - freq))
    return ((d_ref[...].astype(jnp.float32) - 2.0 * freq) * scale).astype(jnp.bfloat16)


def sketch_kernel(me_ref, d_ref, f_ref, p_ref, hl_ref, packed_ref, a_ref):
    k = p_ref.shape[1]
    c = centre(d_ref, f_ref)
    sketch = jnp.dot(c, p_ref[...], preferred_element_type=jnp.float32)
    hi = sketch.astype(jnp.bfloat16)
    lo = (sketch - hi.astype(jnp.float32)).astype(jnp.bfloat16)
    hl_ref[:, :k] = hi
    hl_ref[:, k:] = lo
    i = pl.program_id(0)

    @pl.when(i == 0)
    def _():
        a_ref[...] = dot(hi, hl_ref[...], TN)

    @pl.when(i > 0)
    def _():
        a_ref[...] += dot(hi, hl_ref[...], TN)

    @pl.when(i == pl.num_programs(0) - 1)
    def _():
        def block(p, q):
            r, t = slice(p * B, (p + 1) * B), slice(q * B, (q + 1) * B)
            u, v = slice(k + p * B, k + (p + 1) * B), slice(k + q * B, k + (q + 1) * B)
            return a_ref[r, t] + (a_ref[r, v] + a_ref[t, u].T)

        first = me_ref[0] == 0
        for n in range(HALF):
            a, b = block(*PAIRS[n]), block(*PAIRS[n + HALF])
            near, far = jnp.where(first, a, b), jnp.where(first, b, a)
            for t in range(B // 8):
                chunk, row = divmod(n * (B // 8) + t, ROWS // 8)
                packed_ref[chunk, 8 * row : 8 * row + 8, :] = near[8 * t : 8 * t + 8]
                packed_ref[chunk, ROWS + 8 * row : ROWS + 8 * row + 8, :] = far[8 * t : 8 * t + 8]


def sketch_gram(me, dosage, freq, probes, step=512):
    n, m = dosage.shape
    k = probes.shape[1]
    whole = lambda i: (0, 0)
    return pl.pallas_call(
        sketch_kernel,
        grid=(n // step,),
        in_specs=[
            pl.BlockSpec(memory_space=pltpu.SMEM),
            pl.BlockSpec((step, m), lambda i: (i, 0)),
            pl.BlockSpec((1, m), whole),
            pl.BlockSpec((m, k), whole),
        ],
        out_specs=(
            pl.BlockSpec((step, 2 * k), lambda i: (i, 0)),
            pl.BlockSpec((NX * NY, NC * ROWS, B), lambda i: (0, 0, 0)),
        ),
        out_shape=(
            jax.ShapeDtypeStruct((n, 2 * k), jnp.bfloat16),
            jax.ShapeDtypeStruct((NX * NY, NC * ROWS, B), jnp.float32),
        ),
        scratch_shapes=[pltpu.VMEM((k, 2 * k), jnp.float32)],
        name="sketch_gram",
    )(me, dosage, freq, probes)


def product_kernel(d_ref, f_ref, hl_ref, w_ref):
    k = hl_ref.shape[1] // 2
    c = centre(d_ref, f_ref)
    both = dot(c, hl_ref[...], TN)
    for t in range(NB):
        at, below = slice(t * B, (t + 1) * B), slice(k + t * B, k + (t + 1) * B)
        w_ref[:, t, :] = both[:, at] + both[:, below]


def product(dosage, freq, hl, step=512):
    n, m = dosage.shape
    k = hl.shape[1] // 2
    return pl.pallas_call(
        product_kernel,
        grid=(m // step,),
        in_specs=[
            pl.BlockSpec((n, step), lambda i: (0, i)),
            pl.BlockSpec((1, step), lambda i: (0, i)),
            pl.BlockSpec((n, 2 * k), lambda i: (0, 0)),
        ],
        out_specs=pl.BlockSpec((step, NB, B), lambda i: (i, 0, 0)),
        out_shape=jax.ShapeDtypeStruct((m, NB, B), jnp.float32),
        name="product",
        cost_estimate=pl.CostEstimate(
            flops=4 * n * m * k, bytes_accessed=16 << 20, transcendentals=0
        ),
    )(dosage, freq, hl)


def gather_kernel(flip, me_ref, i_ref, w_ref, *refs):
    o_ref = refs[-1]
    c = (me_ref[0] + flip) & 1

    def block(n, _):
        base = 32 * ((n & 7) * (NY * NC) + ((n >> 3) & 3) * NC + c) + 8 * (n >> 5)
        for s in range(8):
            row = w_ref[i_ref[base + s]]
            o_ref[n * 8 + s] = row if flip else row + refs[0][n * 8 + s]
        return 0

    lax.fori_loop(0, NX * NY * NZ, block, 0, unroll=4)


def gather_rows(flip, me, perm, rows, *came):
    sm, vm = pl.BlockSpec(memory_space=pltpu.SMEM), pl.BlockSpec(memory_space=pltpu.VMEM)
    return pl.pallas_call(
        functools.partial(gather_kernel, flip),
        out_shape=jax.ShapeDtypeStruct((rows.shape[0] // NC,) + rows.shape[1:], rows.dtype),
        in_specs=[sm, sm, vm] + [vm] * len(came),
        out_specs=vm,
        cost_estimate=pl.CostEstimate(flops=6_000_000_000, bytes_accessed=8 << 20, transcendentals=0),
    )(me, perm, rows, *came)


HI = lax.Precision.HIGHEST
NT = (((1,), (1,)), ((), ()))


def factor_kernel(p, me_ref, near_ref, far_ref, *refs):
    prior = refs[:p]
    r_ref, inv_ref, s_ref = refs[p:]
    w = (NB - p) * B
    wide = w + B
    for t in range(NB - p):
        n = PAIRS.index((p, p + t))
        at = slice(n % HALF * B, (n % HALF + 1) * B)
        near = (n // HALF + me_ref[0]) & 1 == 0
        s_ref[:, t * B : (t + 1) * B] = jnp.where(near, near_ref[at, :], far_ref[at, :])
    for q in range(p):
        off = (p - q) * B
        s_ref[:, :w] -= lax.dot_general(
            prior[q][:, off : off + B], prior[q][:, off:], TN,
            precision=HI, preferred_element_type=jnp.float32)
    s_ref[:, w:] = (
        lax.broadcasted_iota(jnp.int32, (B, B), 0) == lax.broadcasted_iota(jnp.int32, (B, B), 1)
    ).astype(jnp.float32)
    ready = None
    for b in range(B // 8):
        lo = 8 * b
        if b and b % G8 == 0:
            done = slice(lo - 8 * G8, lo)
            lead = r_ref[done, :B]
            s_ref[lo:, :w] -= lax.dot_general(
                lead[:, lo:], r_ref[done, :], TN, precision=HI, preferred_element_type=jnp.float32)
            s_ref[lo:, w:] -= lax.dot_general(
                lead[:, lo:], inv_ref[done, :], TN, precision=HI, preferred_element_type=jnp.float32)
        rows = s_ref[lo : lo + 8, :] if ready is None else ready
        ready = None
        cols = [jnp.broadcast_to(rows[:, lo + m : lo + m + 1], (8, B)) for m in range(8)]
        e = [[jnp.broadcast_to(cols[m][j : j + 1, :], (8, B)) if j >= m else None
              for m in range(8)] for j in range(8)]
        u = [[jnp.broadcast_to(rows[j : j + 1, t * B : (t + 1) * B], (8, B))
              for t in range(wide // B)] for j in range(8)]
        inv = [None] * 8
        l = [[None] * 8 for _ in range(8)]
        for j in range(8):
            inv[j] = 1.0 / e[j][j]
            for m in range(j + 1, 8):
                l[m][j] = e[m][j] * inv[j]
            for m in range(j + 1, 8):
                for n in range(m, 8):
                    e[n][m] = e[n][m] - l[n][j] * e[m][j]
                u[m] = [a - l[m][j] * c for a, c in zip(u[m], u[j])]
        v = [[a * inv[j] for a in u[j]] for j in range(8)]
        for j in range(8):
            root = lax.rsqrt(e[j][j])
            root = root * (1.5 - 0.5 * e[j][j] * root * root)
            for t in range(wide // B):
                row = (u[j][t] * root)[0:1, :]
                if t < NB - p:
                    r_ref[lo + j : lo + j + 1, t * B : (t + 1) * B] = row
                else:
                    inv_ref[lo + j : lo + j + 1, :] = row
        for d in range(b + 1, (b // G8 + 1) * G8):
            at = slice(8 * d, 8 * d + 8)
            tail = s_ref[at, :]
            cols = [jnp.broadcast_to(tail[:, lo + m : lo + m + 1], (8, B)) for m in range(8)]
            for j in range(8):
                for m in range(j + 1, 8):
                    cols[m] = cols[m] - cols[j] * l[m][j]
            fresh = []
            for t in range(wide // B):
                x = tail[:, t * B : (t + 1) * B]
                y = cols[0] * v[0][t]
                z = cols[1] * v[1][t]
                for m in range(2, 8, 2):
                    y = y + cols[m] * v[m][t]
                    z = z + cols[m + 1] * v[m + 1][t]
                fresh.append(x - (y + z))
            if d == b + 1:
                ready = jnp.concatenate(fresh, axis=1)
            else:
                s_ref[at, :] = jnp.concatenate(fresh, axis=1)


def factor(p, me, near, far, prior):
    w = (NB - p) * B
    vm = pl.BlockSpec(memory_space=pltpu.VMEM)
    return pl.pallas_call(
        functools.partial(factor_kernel, p),
        out_shape=(
            jax.ShapeDtypeStruct((B, w), jnp.float32),
            jax.ShapeDtypeStruct((B, B), jnp.float32),
        ),
        in_specs=[pl.BlockSpec(memory_space=pltpu.SMEM)] + [vm] * (2 + p),
        out_specs=(vm, vm),
        scratch_shapes=[pltpu.VMEM((B, w + B), jnp.float32)],
        cost_estimate=pl.CostEstimate(flops=10_000_000_000, bytes_accessed=1 << 20, transcendentals=0),
    )(me, near, far, *prior)


def invert_kernel(*refs):
    r, inv, t_ref = refs[:NB], refs[NB : 2 * NB], refs[2 * NB]
    t_ref[...] = jnp.zeros_like(t_ref)
    for p in range(NB):
        at = slice(p * B, (p + 1) * B)
        t_ref[at, at] = inv[p][...].T
        if p:
            strip = jnp.concatenate(
                [r[k][:, (p - k) * B : (p - k + 1) * B] for k in range(p)], axis=0)
            strip = jnp.dot(t_ref[: p * B, : p * B], strip, precision=HI,
                            preferred_element_type=jnp.float32)
            t_ref[: p * B, at] = -lax.dot_general(
                strip, inv[p][...], NT, precision=HI, preferred_element_type=jnp.float32)


def invert(panels, inverses):
    vm = pl.BlockSpec(memory_space=pltpu.VMEM)
    return pl.pallas_call(
        invert_kernel,
        out_shape=jax.ShapeDtypeStruct((NB * B, NB * B), jnp.float32),
        in_specs=[vm] * (2 * NB),
        out_specs=vm,
        name="invert",
    )(*panels, *inverses)


def finish_kernel(w_ref, t_ref, x_ref, s_ref):
    n = x_ref.shape[0]
    rows = w_ref[:, 0]
    for z in range(1, w_ref.shape[1]):
        rows = rows + w_ref[:, z]
    s_ref[...] = rows.reshape(s_ref.shape)
    acc = None
    for t in range(NB):
        part = jnp.dot(s_ref[pl.ds(t, n, stride=NB), :], t_ref[t * B : (t + 1) * B, :],
                       precision=HI, preferred_element_type=jnp.float32)
        acc = part if acc is None else acc + part
    x_ref[...] = acc


def finish(parts, inverse):
    vm = pl.BlockSpec(memory_space=pltpu.VMEM)
    lines = parts.shape[0] * parts.shape[2]
    return pl.pallas_call(
        finish_kernel,
        out_shape=jax.ShapeDtypeStruct((lines // NB, NB * B), jnp.float32),
        in_specs=[vm] * 2,
        out_specs=vm,
        scratch_shapes=[pltpu.VMEM((lines, B), jnp.float32)],
        name="finish",
    )(parts, inverse)


def shifted(value, axis, size, step):
    return lax.ppermute(value, axis, [(k, (k + step) % size) for k in range(size)])


def swap(value, axes):
    return lax.all_to_all(value, axes, 0, 0, tiled=True)


def copies(value, count):
    return jnp.broadcast_to(value[None], (count,) + value.shape)


def after(value, *others):
    return lax.optimization_barrier((value,) + others)


def steps(dosage, allele_freq, probes, owner_perm):
    c = lax.axis_index("c")
    me = jnp.full((1,), c, jnp.int32)
    freq = allele_freq[None, :]
    both, packed = sketch_gram(me, dosage, freq, probes)
    part = swap(packed, ("x", "y"))
    rows = product(dosage, freq, both)
    part, rows = after(part.sum(0), rows)
    part = part[:ROWS] + shifted(part[ROWS:], "c", NC, 1)
    part = swap(copies(part, NZ), "z")
    away = gather_rows(1, me, owner_perm, rows)
    part, away = after(part.sum(0), away)
    came = shifted(away, "c", NC, 1)
    near = swap(copies(part, NX * NY), ("x", "y")).reshape(-1, B)
    kept = gather_rows(0, me, owner_perm, rows, came)
    near, kept = after(near, kept)
    far = shifted(near, "c", NC, 1)
    owned = swap(kept.reshape(NX * NY, -1, B), ("x", "y"))
    panels, inverses = [], []
    for p in range(NB):
        r, inv = factor(p, me, near, far, panels)
        panels.append(r)
        inverses.append(inv)
    owned = owned.sum(0).reshape(NZ, -1, B)
    owned = swap(copies(owned, NX).reshape(NX * NZ, -1, B), ("x", "z"))
    inverse = invert(panels, inverses)
    return finish(owned.reshape(NX, NZ, -1, B), inverse)


def solution(mesh):
    torus = Mesh(mesh.devices.reshape(NX, NZ, NY, NC), ("x", "z", "y", "c"))
    return jax.shard_map(
        steps,
        mesh=torus,
        in_specs=(P(("x", "z", "y", "c"), None), P(), P(), P()),
        out_specs=P(("z", "y", "c"), None),
        check_vma=False,
    )
```

profile of v0, /device:TPU:8, one launch (start us, length us, event | category | flops | bytes accessed | tf_op | source)
XLA Modules:
  0.0 133.0 jit_solution(1809898664329258304)
XLA Ops:
  0.0 11.9 %sketch_gram.1 = (bf16[2048,1024]{1,0:T(8,128)(2,1)}, f32[16,80,128]{2,1,0:T(8,128)}) custom-call(s32[1]{0:T(128)} %bitcast.me_ref, bf16[2048,2048]{1,0:T(8,128)(2,1)} %d_ref.3, f32[1,2048]{1,0:T(1,128)} %bitcast.15, bf16[2048,512]{1,0:T(8,128)(2,1)} %p_ref.1), custom_call_target="tpu_custom_call" | custom-call | tf_op jit(solution)/shard_map/sketch_gram/pallas_call | solution.py:71
  11.9 7.4 %all-to-all-start = ((f32[16,80,128]{2,1,0:T(8,128)}), f32[16,80,128]{2,1,0:T(8,128)S(1)}, u32[]{:S(2)}, u32[]{:S(2)}) async-start(f32[16,80,128]{2,1,0:T(8,128)} %get-tuple-element.21), calls=%async_computation | async-start | bytes 1310720 | tf_op jit(solution)/shard_map/all_to_all | solution.py:302
  19.3 15.2 %product.1.w_ref = f32[2048,4,128]{2,1,0:T(4,128)} custom-call(bf16[2048,2048]{1,0:T(8,128)(2,1)} %d_ref.3, f32[1,2048]{1,0:T(1,128)} %bitcast.16, bf16[2048,1024]{1,0:T(8,128)(2,1)} %get-tuple-element.22.hl_ref), custom_call_target="tpu_custom_call" | custom-call | flops 8589934592 | bytes 16777216 | tf_op jit(solution)/shard_map/product/pallas_call | solution.py:105
  34.5 0.0 all-to-all-done
  34.5 0.1 collective-permute-start
  34.6 1.2 collective-permute-done
  35.8 0.7 broadcast_in_dim.27
  36.5 8.5 %all-to-all-start.1 = ((f32[8,40,128]{2,1,0:T(8,128)}), f32[8,40,128]{2,1,0:T(8,128)S(1)}, u32[]{:S(2)}, u32[]{:S(2)}) async-start(f32[8,40,128]{2,1,0:T(8,128)} %broadcast_in_dim.27), calls=%async_computation.1 | async-start | bytes 327680 | tf_op jit(solution)/shard_map/all_to_all | solution.py:302
  45.0 5.1 %shard_map.46 = f32[1024,4,128]{2,1,0:T(4,128)} custom-call(s32[1]{0:T(128)} %bitcast.me_ref, s32[2048]{0:T(1024)} %i_ref.3, f32[2048,4,128]{2,1,0:T(4,128)} %product.1.w_ref), custom_call_target="tpu_custom_call" | custom-call | flops 6000000000 | bytes 8388608 | tf_op jit(solution)/shard_map/pallas_call | solution.py:138
  50.1 5.0 %all-to-all-done.1 = f32[8,40,128]{2,1,0:T(8,128)S(1)} async-done(((f32[8,40,128]{2,1,0:T(8,128)}), f32[8,40,128]{2,1,0:T(8,128)S(1)}, u32[]{:S(2)}, u32[]{:S(2)}) %all-to-all-start.1) | async-done | bytes 163872 | tf_op jit(solution)/shard_map/all_to_all | solution.py:302
  55.1 0.1 collective-permute-start.1
  55.2 0.8 broadcast_in_dim.28
  55.9 7.2 %all-to-all-start.2 = ((f32[16,40,128]{2,1,0:T(8,128)}), f32[16,40,128]{2,1,0:T(8,128)S(1)}, u32[]{:S(2)}, u32[]{:S(2)}) async-start(f32[16,40,128]{2,1,0:T(8,128)} %broadcast_in_dim.28), calls=%async_computation.2 | async-start | bytes 655360 | tf_op jit(solution)/shard_map/all_to_all | solution.py:302
  63.2 0.0 collective-permute-done.1.refs_0_
  63.2 5.9 %shard_map.47 = f32[1024,4,128]{2,1,0:T(4,128)} custom-call(s32[1]{0:T(128)} %bitcast.me_ref, s32[2048]{0:T(1024)} %i_ref.3, f32[2048,4,128]{2,1,0:T(4,128)} %product.1.w_ref, f32[1024,4,128]{2,1,0:T(4,128)} %collective-permute-done.1.refs_0_), custom_call_target="tpu_custom_call" | custom-call | flops 6000000000 | bytes 8388608 | tf_op jit(solution)/shard_map/pallas_call | solution.py:138
  69.0 2.4 %all-to-all-done.2 = f32[16,40,128]{2,1,0:T(8,128)S(1)} async-done(((f32[16,40,128]{2,1,0:T(8,128)}), f32[16,40,128]{2,1,0:T(8,128)S(1)}, u32[]{:S(2)}, u32[]{:S(2)}) %all-to-all-start.2) | async-done | bytes 327712 | tf_op jit(solution)/shard_map/all_to_all | solution.py:302
  71.4 0.0 collective-permute-start.2
  71.4 0.7 copy-done.1
  72.1 5.3 %all-to-all-start.3 = ((f32[16,256,128]{2,1,0:T(8,128)}), f32[16,256,128]{2,1,0:T(8,128)S(1)}, u32[]{:S(2)}, u32[]{:S(2)}) async-start(f32[16,256,128]{2,1,0:T(8,128)} %bitcast.8), calls=%async_computation.3 | async-start | bytes 4194304 | tf_op jit(solution)/shard_map/all_to_all | solution.py:302
  77.4 0.0 collective-permute-done.2.far_ref
  77.4 0.7 copy-done.2
  78.1 6.4 %shard_map.48 = (f32[128,512]{1,0:T(8,128)}, f32[128,128]{1,0:T(8,128)}) custom-call(s32[1]{0:T(128)} %bitcast.me_ref, f32[640,128]{1,0:T(8,128)} %bitcast.11, f32[640,128]{1,0:T(8,128)} %copy-done.2), custom_call_target="tpu_custom_call" | custom-call | flops 10000000000 | bytes 1048576 | tf_op jit(solution)/shard_map/pallas_call | solution.py:231
  84.5 6.7 %shard_map.49 = (f32[128,384]{1,0:T(8,128)}, f32[128,128]{1,0:T(8,128)}) custom-call(s32[1]{0:T(128)} %bitcast.me_ref, f32[640,128]{1,0:T(8,128)} %bitcast.12, f32[640,128]{1,0:T(8,128)} %copy-done.2, f32[128,512]{1,0:T(8,128)} %get-tuple-element.29.refs_0_), custom_call_target="tpu_custom_call" | custom-call | flops 10000000000 | bytes 1048576 | tf_op jit(solution)/shard_map/pallas_call | solution.py:231
  91.2 15.6 %all-to-all-done.3 = f32[16,256,128]{2,1,0:T(8,128)S(1)} async-done(((f32[16,256,128]{2,1,0:T(8,128)}), f32[16,256,128]{2,1,0:T(8,128)S(1)}, u32[]{:S(2)}, u32[]{:S(2)}) %all-to-all-start.3) | async-done | bytes 2097184 | tf_op jit(solution)/shard_map/all_to_all | solution.py:302
  106.9 0.1 reduce_sum.29
  107.0 0.9 broadcast_in_dim.30
  107.9 4.1 %all-to-all-start.4 = ((f32[32,32,128]{2,1,0:T(8,128)}), f32[32,32,128]{2,1,0:T(8,128)S(1)}, u32[]{:S(2)}, u32[]{:S(2)}) async-start(f32[32,32,128]{2,1,0:T(8,128)} %bitcast.5), calls=%async_computation.4 | async-start | bytes 1048576 | tf_op jit(solution)/shard_map/all_to_all | solution.py:302
  112.0 6.6 %shard_map.50 = (f32[128,256]{1,0:T(8,128)}, f32[128,128]{1,0:T(8,128)}) custom-call(s32[1]{0:T(128)} %bitcast.me_ref, f32[640,128]{1,0:T(8,128)} %bitcast.13, f32[640,128]{1,0:T(8,128)} %copy-done.2, f32[128,512]{1,0:T(8,128)} %get-tuple-element.29.refs_0_, f32[128,384]{1,0:T(8,128)} %get-tuple-element.30.refs_1_), custom_call_target="tpu_custom_call" | custom-call | flops 10000000000 | bytes 1048576 | tf_op jit(solution)/shard_map/pallas_call | solution.py:231
  118.6 6.5 %shard_map.51 = (f32[128,128]{1,0:T(8,128)}, f32[128,128]{1,0:T(8,128)}) custom-call(s32[1]{0:T(128)} %bitcast.me_ref, f32[640,128]{1,0:T(8,128)} %bitcast.14, f32[640,128]{1,0:T(8,128)} %copy-done.2, f32[128,512]{1,0:T(8,128)} %get-tuple-element.29.refs_0_, f32[128,384]{1,0:T(8,128)} %get-tuple-element.30.refs_1_, f32[128,256]{1,0:T(8,128)} %get-tuple-element.31.refs_2_), custom_call_target="tpu_custom_call" | custom-call | flops 10000000000 | bytes 1048576 | tf_op jit(solution)/shard_map/pallas_call | solution.py:231
  125.1 4.5 %invert.1.t_ref = f32[512,512]{1,0:T(8,128)} custom-call(f32[128,512]{1,0:T(8,128)} %get-tuple-element.29.refs_0_, f32[128,384]{1,0:T(8,128)} %get-tuple-element.30.refs_1_, f32[128,256]{1,0:T(8,128)} %get-tuple-element.31.refs_2_, f32[128,128]{1,0:T(8,128)} %get-tuple-element.32.refs_3_, f32[128,128]{1,0:T(8,128)} %get-tuple-element.33.refs_4_, ...), custom_call_target="tpu_custom_call" | custom-call | tf_op jit(solution)/shard_map/invert/pallas_call | solution.py:261
  129.6 0.8 copy-done
  130.4 2.6 %finish.1 = f32[32,512]{1,0:T(8,128)} custom-call(f32[4,8,32,128]{3,2,1,0:T(8,128)} %bitcast.7, f32[512,512]{1,0:T(8,128)} %invert.1.t_ref), custom_call_target="tpu_custom_call" | custom-call | tf_op jit(solution)/shard_map/finish/pallas_call | solution.py:287
  (8 shorter events, 0.1 us)
Async XLA Ops:
  11.9 22.6 %all-to-all-start = ((f32[16,80,128]{2,1,0:T(8,128)}), f32[16,80,128]{2,1,0:T(8,128)S(1)}, u32[]{:S(2)}, u32[]{:S(2)}) async-start(f32[16,80,128]{2,1,0:T(8,128)} %get-tuple-element.21), calls=%async_computation | async-start | bytes 1310720 | tf_op jit(solution)/shard_map/all_to_all | solution.py:302
  34.5 1.3 collective-permute-start
  36.5 18.6 %all-to-all-start.1 = ((f32[8,40,128]{2,1,0:T(8,128)}), f32[8,40,128]{2,1,0:T(8,128)S(1)}, u32[]{:S(2)}, u32[]{:S(2)}) async-start(f32[8,40,128]{2,1,0:T(8,128)} %broadcast_in_dim.27), calls=%async_computation.1 | async-start | bytes 327680 | tf_op jit(solution)/shard_map/all_to_all | solution.py:302
  55.1 8.1 %collective-permute-start.1 = (f32[1024,4,128]{2,1,0:T(4,128)}, f32[1024,4,128]{2,1,0:T(4,128)}, u32[]{:S(2)}, u32[]{:S(2)}) collective-permute-start(f32[1024,4,128]{2,1,0:T(4,128)} %shard_map.46), channel_id=1, source_target_pairs={{0,1},{1,0},{2,3},{3,2},{4,5},{5,4},{6,7},{7,6},{8,9},{9,8},{10,11... | collective-permute-start | bytes 6291464 | tf_op jit(solution)/shard_map/ppermute | solution.py:298
  55.9 15.5 %all-to-all-start.2 = ((f32[16,40,128]{2,1,0:T(8,128)}), f32[16,40,128]{2,1,0:T(8,128)S(1)}, u32[]{:S(2)}, u32[]{:S(2)}) async-start(f32[16,40,128]{2,1,0:T(8,128)} %broadcast_in_dim.28), calls=%async_computation.2 | async-start | bytes 655360 | tf_op jit(solution)/shard_map/all_to_all | solution.py:302
  71.4 0.7 copy-start.1
  71.4 6.0 %collective-permute-start.2 = (f32[640,128]{1,0:T(8,128)S(1)}, f32[640,128]{1,0:T(8,128)S(1)}, u32[]{:S(2)}, u32[]{:S(2)}) collective-permute-start(f32[640,128]{1,0:T(8,128)S(1)} %bitcast.10), channel_id=1, source_target_pairs={{0,1},{1,0},{2,3},{3,2},{4,5},{5,4},{6,7},{7,6},{8,9},{9,8},{10,11... | collective-permute-start | bytes 983048 | tf_op jit(solution)/shard_map/ppermute | solution.py:298
  72.1 34.8 %all-to-all-start.3 = ((f32[16,256,128]{2,1,0:T(8,128)}), f32[16,256,128]{2,1,0:T(8,128)S(1)}, u32[]{:S(2)}, u32[]{:S(2)}) async-start(f32[16,256,128]{2,1,0:T(8,128)} %bitcast.8), calls=%async_computation.3 | async-start | bytes 4194304 | tf_op jit(solution)/shard_map/all_to_all | solution.py:302
  77.4 0.7 copy-start.2
  107.9 21.7 %all-to-all-start.4 = ((f32[32,32,128]{2,1,0:T(8,128)}), f32[32,32,128]{2,1,0:T(8,128)S(1)}, u32[]{:S(2)}, u32[]{:S(2)}) async-start(f32[32,32,128]{2,1,0:T(8,128)} %bitcast.5), calls=%async_computation.4 | async-start | bytes 1048576 | tf_op jit(solution)/shard_map/all_to_all | solution.py:302
  129.6 0.8 copy-start
where the time goes:
time: 135 us; the launch traced here: 133 us
  Pallas kernels  71.5 us (53%)
  starting transfers between devices  32.6 us (24%)
  waiting for transfers between devices  24.1 us (18%)
  local copies, waits for them, and re-layouts  4.54 us (3%)
    all_to_all x5, starting transfers between devices, swap(): return lax.all_to_all(value, axes, 0, 0, tiled=True)  32.5 us
    pallas_call x4, Pallas kernels, factor(): pl.pallas_call(functools.partial(factor_kernel, p), out_shape=(jax.ShapeD...  26.2 us
    all_to_all x5, waiting for transfers between devices, swap(): return lax.all_to_all(value, axes, 0, 0, tiled=True)  23 us
    pallas_call x1, Pallas kernels, product(): pl.pallas_call(product_kernel, grid=(m // step,), in_specs=[pl.BlockSpec(...  15.2 us
    pallas_call x1, Pallas kernels, sketch_gram(): pl.pallas_call(sketch_kernel, grid=(n // step,), in_specs=[pl.BlockSpec(m...  11.9 us
    pallas_call x2, Pallas kernels, gather_rows(): pl.pallas_call(functools.partial(gather_kernel, flip), out_shape=jax.Shap...  11 us
    pallas_call x1, Pallas kernels, invert(): pl.pallas_call(invert_kernel, out_shape=jax.ShapeDtypeStruct((NB * B, NB...  4.51 us
  transfers between devices with their start and end apart: 8, of which 4 were waited for; matrix products, arithmetic and copies ran while one was open for 1% of the time, Pallas kernels for 43%

commit v1 on v0

--- a/solution.py
+++ b/solution.py
@@ -91,12 +91,10 @@
 
 
 def product_kernel(d_ref, f_ref, hl_ref, w_ref):
-    k = hl_ref.shape[1] // 2
+    k = w_ref.shape[1]
     c = centre(d_ref, f_ref)
     both = dot(c, hl_ref[...], TN)
-    for t in range(NB):
-        at, below = slice(t * B, (t + 1) * B), slice(k + t * B, k + (t + 1) * B)
-        w_ref[:, t, :] = both[:, at] + both[:, below]
+    w_ref[...] = both[:, :k] + both[:, k:]
 
 
 def product(dosage, freq, hl, step=512):
@@ -110,8 +108,8 @@
             pl.BlockSpec((1, step), lambda i: (0, i)),
             pl.BlockSpec((n, 2 * k), lambda i: (0, 0)),
         ],
-        out_specs=pl.BlockSpec((step, NB, B), lambda i: (i, 0, 0)),
-        out_shape=jax.ShapeDtypeStruct((m, NB, B), jnp.float32),
+        out_specs=pl.BlockSpec((step, k), lambda i: (i, 0)),
+        out_shape=jax.ShapeDtypeStruct((m, k), jnp.float32),
         name="product",
         cost_estimate=pl.CostEstimate(
             flops=4 * n * m * k, bytes_accessed=16 << 20, transcendentals=0
@@ -125,9 +123,9 @@
 
     def block(n, _):
         base = 32 * ((n & 7) * (NY * NC) + ((n >> 3) & 3) * NC + c) + 8 * (n >> 5)
-        for s in range(8):
-            row = w_ref[i_ref[base + s]]
-            o_ref[n * 8 + s] = row if flip else row + refs[0][n * 8 + s]
+        at = pl.ds(pl.multiple_of(n * 8, 8), 8)
+        rows = jnp.concatenate([w_ref[pl.ds(i_ref[base + s], 1), :] for s in range(8)], axis=0)
+        o_ref[at, :] = rows if flip else rows + refs[0][at, :]
         return 0
 
     lax.fori_loop(0, NX * NY * NZ, block, 0, unroll=4)
@@ -137,7 +135,7 @@
     sm, vm = pl.BlockSpec(memory_space=pltpu.SMEM), pl.BlockSpec(memory_space=pltpu.VMEM)
     return pl.pallas_call(
         functools.partial(gather_kernel, flip),
-        out_shape=jax.ShapeDtypeStruct((rows.shape[0] // NC,) + rows.shape[1:], rows.dtype),
+        out_shape=jax.ShapeDtypeStruct((rows.shape[0] // NC, rows.shape[1]), rows.dtype),
         in_specs=[sm, sm, vm] + [vm] * len(came),
         out_specs=vm,
         cost_estimate=pl.CostEstimate(flops=6_000_000_000, bytes_accessed=8 << 20, transcendentals=0),
@@ -267,29 +265,21 @@
     )(*panels, *inverses)
 
 
-def finish_kernel(w_ref, t_ref, x_ref, s_ref):
-    n = x_ref.shape[0]
+def finish_kernel(w_ref, t_ref, x_ref):
     rows = w_ref[:, 0]
     for z in range(1, w_ref.shape[1]):
         rows = rows + w_ref[:, z]
-    s_ref[...] = rows.reshape(s_ref.shape)
-    acc = None
-    for t in range(NB):
-        part = jnp.dot(s_ref[pl.ds(t, n, stride=NB), :], t_ref[t * B : (t + 1) * B, :],
-                       precision=HI, preferred_element_type=jnp.float32)
-        acc = part if acc is None else acc + part
-    x_ref[...] = acc
+    x_ref[...] = jnp.dot(rows.reshape(x_ref.shape), t_ref[...], precision=HI,
+                         preferred_element_type=jnp.float32)
 
 
 def finish(parts, inverse):
     vm = pl.BlockSpec(memory_space=pltpu.VMEM)
-    lines = parts.shape[0] * parts.shape[2]
     return pl.pallas_call(
         finish_kernel,
-        out_shape=jax.ShapeDtypeStruct((lines // NB, NB * B), jnp.float32),
+        out_shape=jax.ShapeDtypeStruct((parts.shape[0] * parts.shape[2], parts.shape[3]), jnp.float32),
         in_specs=[vm] * 2,
         out_specs=vm,
-        scratch_shapes=[pltpu.VMEM((lines, B), jnp.float32)],
         name="finish",
     )(parts, inverse)
 
@@ -325,18 +315,18 @@
     came = shifted(away, "c", NC, 1)
     near = swap(copies(part, NX * NY), ("x", "y")).reshape(-1, B)
     kept = gather_rows(0, me, owner_perm, rows, came)
-    near, kept = after(near, kept)
     far = shifted(near, "c", NC, 1)
-    owned = swap(kept.reshape(NX * NY, -1, B), ("x", "y"))
+    k = rows.shape[1]
+    owned = swap(kept.reshape(NX * NY, -1, k), ("x", "y"))
     panels, inverses = [], []
     for p in range(NB):
         r, inv = factor(p, me, near, far, panels)
         panels.append(r)
         inverses.append(inv)
-    owned = owned.sum(0).reshape(NZ, -1, B)
-    owned = swap(copies(owned, NX).reshape(NX * NZ, -1, B), ("x", "z"))
+    owned = owned.sum(0).reshape(NZ, -1, k)
+    owned = swap(copies(owned, NX).reshape(NX * NZ, -1, k), ("x", "z"))
     inverse = invert(panels, inverses)
-    return finish(owned.reshape(NX, NZ, -1, B), inverse)
+    return finish(owned.reshape(NX, NZ, -1, k), inverse)
 
 
 def solution(mesh):

time: 135 us -> 140 us (1.037)
  blocking collectives: 0 us -> 15.3 us
  starting transfers between devices: 32.6 us -> 26.7 us
  waiting for transfers between devices: 24.1 us -> 20.8 us
    all_to_all x0 -> x1, blocking collectives: none -> 15.3 us  [swap(): return lax.all_to_all(value, axes, 0, 0, tiled=True)]
    all_to_all x5 -> x4, starting transfers between devices: 32.5 us -> 26.5 us  [swap(): return lax.all_to_all(value, axes, 0, 0, tiled=True)]
    all_to_all x5 -> x4, waiting for transfers between devices: 23 us -> 19.6 us  [swap(): return lax.all_to_all(value, axes, 0, 0, tiled=True)]
    pallas_call x2, Pallas kernels: 11 us -> 13.1 us  [gather_rows(): pl.pallas_call(functools.partial(gather_kernel, flip), out_shape=jax.Shap...]
    pallas_call x1, Pallas kernels: 15.2 us -> 13.4 us  [product(): pl.pallas_call(product_kernel, grid=(m // step,), in_specs=[pl.BlockSpec(...]
  transfers between devices with their start and end apart: 8 -> 7, of which waited for: 4 -> 3; matrix products, arithmetic and copies ran while one was open for 1% -> 0% of each run, Pallas kernels for 43% -> 42%
where the time goes in v1:
time: 140 us; the launch traced here: 138 us
  Pallas kernels  71.9 us (51%)
  starting transfers between devices  26.7 us (19%)
  waiting for transfers between devices  20.8 us (15%)
  blocking collectives  15.3 us (11%)
  local copies, waits for them, and re-layouts  3.16 us (2%)
    all_to_all x4, starting transfers between devices, swap(): return lax.all_to_all(value, axes, 0, 0, tiled=True)  26.5 us
    pallas_call x4, Pallas kernels, factor(): pl.pallas_call(functools.partial(factor_kernel, p), out_shape=(jax.ShapeD...  26.2 us
    all_to_all x4, waiting for transfers between devices, swap(): return lax.all_to_all(value, axes, 0, 0, tiled=True)  19.6 us
    all_to_all x1, blocking collectives, swap(): return lax.all_to_all(value, axes, 0, 0, tiled=True)  15.3 us
    pallas_call x1, Pallas kernels, product(): pl.pallas_call(product_kernel, grid=(m // step,), in_specs=[pl.BlockSpec(...  13.4 us
    pallas_call x2, Pallas kernels, gather_rows(): pl.pallas_call(functools.partial(gather_kernel, flip), out_shape=jax.Shap...  13.1 us
    pallas_call x1, Pallas kernels, sketch_gram(): pl.pallas_call(sketch_kernel, grid=(n // step,), in_specs=[pl.BlockSpec(m...  11.9 us
    pallas_call x1, Pallas kernels, invert(): pl.pallas_call(invert_kernel, out_shape=jax.ShapeDtypeStruct((NB * B, NB...  4.51 us
  transfers between devices with their start and end apart: 7, of which 3 were waited for; matrix products, arithmetic and copies ran while one was open for 0% of the time, Pallas kernels for 42%

profile of v1, /device:TPU:8, one launch (start us, length us, event | category | flops | bytes accessed | tf_op | source)
XLA Modules:
  0.0 138.0 jit_solution(17770268646991540508)
XLA Ops:
  0.0 11.9 %sketch_gram.1 = (bf16[2048,1024]{1,0:T(8,128)(2,1)}, f32[16,80,128]{2,1,0:T(8,128)}) custom-call(s32[1]{0:T(128)} %bitcast.me_ref, bf16[2048,2048]{1,0:T(8,128)(2,1)} %d_ref.3, f32[1,2048]{1,0:T(1,128)} %bitcast.15, bf16[2048,512]{1,0:T(8,128)(2,1)} %p_ref.1), custom_call_target="tpu_custom_call" | custom-call | tf_op jit(solution)/shard_map/sketch_gram/pallas_call | solution.py:71
  11.9 7.4 %all-to-all-start = ((f32[16,80,128]{2,1,0:T(8,128)}), f32[16,80,128]{2,1,0:T(8,128)S(1)}, u32[]{:S(2)}, u32[]{:S(2)}) async-start(f32[16,80,128]{2,1,0:T(8,128)} %get-tuple-element.19), calls=%async_computation | async-start | bytes 1310720 | tf_op jit(solution)/shard_map/all_to_all | solution.py:292
  19.3 13.4 %product.1.w_ref = f32[2048,512]{1,0:T(8,128)} custom-call(bf16[2048,2048]{1,0:T(8,128)(2,1)} %d_ref.3, f32[1,2048]{1,0:T(1,128)} %bitcast.16, bf16[2048,1024]{1,0:T(8,128)(2,1)} %get-tuple-element.20.hl_ref), custom_call_target="tpu_custom_call" | custom-call | flops 8589934592 | bytes 16777216 | tf_op jit(solution)/shard_map/product/pallas_call | solution.py:103
  32.7 0.0 all-to-all-done
  32.7 0.1 collective-permute-start
  32.8 1.2 collective-permute-done
  34.0 0.7 broadcast_in_dim.27
  34.7 8.5 %all-to-all-start.1 = ((f32[8,40,128]{2,1,0:T(8,128)}), f32[8,40,128]{2,1,0:T(8,128)S(1)}, u32[]{:S(2)}, u32[]{:S(2)}) async-start(f32[8,40,128]{2,1,0:T(8,128)} %broadcast_in_dim.27), calls=%async_computation.1 | async-start | bytes 327680 | tf_op jit(solution)/shard_map/all_to_all | solution.py:292
  43.2 6.2 %shard_map.46 = f32[1024,512]{1,0:T(8,128)} custom-call(s32[1]{0:T(128)} %bitcast.me_ref, s32[2048]{0:T(1024)} %i_ref.3, f32[2048,512]{1,0:T(8,128)} %product.1.w_ref), custom_call_target="tpu_custom_call" | custom-call | flops 6000000000 | bytes 8388608 | tf_op jit(solution)/shard_map/pallas_call | solution.py:136
  49.3 3.9 %all-to-all-done.1 = f32[8,40,128]{2,1,0:T(8,128)S(1)} async-done(((f32[8,40,128]{2,1,0:T(8,128)}), f32[8,40,128]{2,1,0:T(8,128)S(1)}, u32[]{:S(2)}, u32[]{:S(2)}) %all-to-all-start.1) | async-done | bytes 163872 | tf_op jit(solution)/shard_map/all_to_all | solution.py:292
  53.3 0.1 collective-permute-start.1
  53.4 15.3 %all_to_all.25 = f32[16,40,128]{2,1,0:T(8,128)S(1)} all-to-all(f32[16,40,128]{2,1,0:T(8,128)S(1)} %broadcast_in_dim.30), channel_id=1, replica_groups=mesh['x'=4,'z'=8,'y'=4,'c'=2] {'x','y'}, dimensions={0} | all-to-all | bytes 655360 | tf_op jit(solution)/shard_map/all_to_all | solution.py:292
  68.7 0.0 collective-permute-start.2
  68.7 0.0 collective-permute-done.1.refs_0_
  68.7 7.0 %shard_map.47 = f32[1024,512]{1,0:T(8,128)} custom-call(s32[1]{0:T(128)} %bitcast.me_ref, s32[2048]{0:T(1024)} %i_ref.3, f32[2048,512]{1,0:T(8,128)} %product.1.w_ref, f32[1024,512]{1,0:T(8,128)} %collective-permute-done.1.refs_0_), custom_call_target="tpu_custom_call" | custom-call | flops 6000000000 | bytes 8388608 | tf_op jit(solution)/shard_map/pallas_call | solution.py:136
  75.7 0.0 copy-done.1
  75.7 5.3 %all-to-all-start.2 = ((f32[16,64,512]{2,1,0:T(8,128)}), f32[16,64,512]{2,1,0:T(8,128)S(1)}, u32[]{:S(2)}, u32[]{:S(2)}) async-start(f32[16,64,512]{2,1,0:T(8,128)} %bitcast.8), calls=%async_computation.2 | async-start | bytes 4194304 | tf_op jit(solution)/shard_map/all_to_all | solution.py:292
  80.9 0.0 collective-permute-done.2.far_ref
  80.9 0.0 copy-start.2
  80.9 0.7 copy-done.2
  81.7 6.4 %shard_map.48 = (f32[128,512]{1,0:T(8,128)}, f32[128,128]{1,0:T(8,128)}) custom-call(s32[1]{0:T(128)} %bitcast.me_ref, f32[640,128]{1,0:T(8,128)} %bitcast.11, f32[640,128]{1,0:T(8,128)} %copy-done.2), custom_call_target="tpu_custom_call" | custom-call | flops 10000000000 | bytes 1048576 | tf_op jit(solution)/shard_map/pallas_call | solution.py:229
  88.1 6.7 %shard_map.49 = (f32[128,384]{1,0:T(8,128)}, f32[128,128]{1,0:T(8,128)}) custom-call(s32[1]{0:T(128)} %bitcast.me_ref, f32[640,128]{1,0:T(8,128)} %bitcast.12, f32[640,128]{1,0:T(8,128)} %copy-done.2, f32[128,512]{1,0:T(8,128)} %get-tuple-element.25.refs_0_), custom_call_target="tpu_custom_call" | custom-call | flops 10000000000 | bytes 1048576 | tf_op jit(solution)/shard_map/pallas_call | solution.py:229
  94.8 15.7 %all-to-all-done.2 = f32[16,64,512]{2,1,0:T(8,128)S(1)} async-done(((f32[16,64,512]{2,1,0:T(8,128)}), f32[16,64,512]{2,1,0:T(8,128)S(1)}, u32[]{:S(2)}, u32[]{:S(2)}) %all-to-all-start.2) | async-done | bytes 2097184 | tf_op jit(solution)/shard_map/all_to_all | solution.py:292
  110.5 0.2 reduce_sum.29
  110.6 0.9 broadcast_in_dim.29
  111.5 5.4 %all-to-all-start.3 = ((f32[32,8,512]{2,1,0:T(8,128)}), f32[32,8,512]{2,1,0:T(8,128)S(1)}, u32[]{:S(2)}, u32[]{:S(2)}) async-start(f32[32,8,512]{2,1,0:T(8,128)} %bitcast.4), calls=%async_computation.3 | async-start | bytes 1048576 | tf_op jit(solution)/shard_map/all_to_all | solution.py:292
  116.9 6.6 %shard_map.50 = (f32[128,256]{1,0:T(8,128)}, f32[128,128]{1,0:T(8,128)}) custom-call(s32[1]{0:T(128)} %bitcast.me_ref, f32[640,128]{1,0:T(8,128)} %bitcast.13, f32[640,128]{1,0:T(8,128)} %copy-done.2, f32[128,512]{1,0:T(8,128)} %get-tuple-element.25.refs_0_, f32[128,384]{1,0:T(8,128)} %get-tuple-element.26.refs_1_), custom_call_target="tpu_custom_call" | custom-call | flops 10000000000 | bytes 1048576 | tf_op jit(solution)/shard_map/pallas_call | solution.py:229
  123.5 6.5 %shard_map.51 = (f32[128,128]{1,0:T(8,128)}, f32[128,128]{1,0:T(8,128)}) custom-call(s32[1]{0:T(128)} %bitcast.me_ref, f32[640,128]{1,0:T(8,128)} %bitcast.14, f32[640,128]{1,0:T(8,128)} %copy-done.2, f32[128,512]{1,0:T(8,128)} %get-tuple-element.25.refs_0_, f32[128,384]{1,0:T(8,128)} %get-tuple-element.26.refs_1_, f32[128,256]{1,0:T(8,128)} %get-tuple-element.27.refs_2_), custom_call_target="tpu_custom_call" | custom-call | flops 10000000000 | bytes 1048576 | tf_op jit(solution)/shard_map/pallas_call | solution.py:229
  130.0 4.5 %invert.1.t_ref = f32[512,512]{1,0:T(8,128)} custom-call(f32[128,512]{1,0:T(8,128)} %get-tuple-element.25.refs_0_, f32[128,384]{1,0:T(8,128)} %get-tuple-element.26.refs_1_, f32[128,256]{1,0:T(8,128)} %get-tuple-element.27.refs_2_, f32[128,128]{1,0:T(8,128)} %get-tuple-element.28.refs_3_, f32[128,128]{1,0:T(8,128)} %get-tuple-element.29.refs_4_, ...), custom_call_target="tpu_custom_call" | custom-call | tf_op jit(solution)/shard_map/invert/pallas_call | solution.py:259
  134.5 0.0 all-to-all-done.3
  134.5 0.8 copy-done
  135.3 2.7 %finish.1 = f32[32,512]{1,0:T(8,128)} custom-call(f32[4,8,8,512]{3,2,1,0:T(8,128)} %bitcast.7, f32[512,512]{1,0:T(8,128)} %invert.1.t_ref), custom_call_target="tpu_custom_call" | custom-call | tf_op jit(solution)/shard_map/finish/pallas_call | solution.py:278
  (7 shorter events, 0.1 us)
Async XLA Ops:
  11.9 20.8 %all-to-all-start = ((f32[16,80,128]{2,1,0:T(8,128)}), f32[16,80,128]{2,1,0:T(8,128)S(1)}, u32[]{:S(2)}, u32[]{:S(2)}) async-start(f32[16,80,128]{2,1,0:T(8,128)} %get-tuple-element.19), calls=%async_computation | async-start | bytes 1310720 | tf_op jit(solution)/shard_map/all_to_all | solution.py:292
  32.7 1.3 collective-permute-start
  34.7 18.6 %all-to-all-start.1 = ((f32[8,40,128]{2,1,0:T(8,128)}), f32[8,40,128]{2,1,0:T(8,128)S(1)}, u32[]{:S(2)}, u32[]{:S(2)}) async-start(f32[8,40,128]{2,1,0:T(8,128)} %broadcast_in_dim.27), calls=%async_computation.1 | async-start | bytes 327680 | tf_op jit(solution)/shard_map/all_to_all | solution.py:292
  53.3 15.4 %collective-permute-start.1 = (f32[1024,512]{1,0:T(8,128)}, f32[1024,512]{1,0:T(8,128)}, u32[]{:S(2)}, u32[]{:S(2)}) collective-permute-start(f32[1024,512]{1,0:T(8,128)} %shard_map.46), channel_id=1, source_target_pairs={{0,1},{1,0},{2,3},{3,2},{4,5},{5,4},{6,7},{7,6},{8,9},{9,8},{10,11... | collective-permute-start | bytes 6291464 | tf_op jit(solution)/shard_map/ppermute | solution.py:288
  68.7 7.0 %copy-start.1 = (f32[16,40,128]{2,1,0:T(8,128)}, f32[16,40,128]{2,1,0:T(8,128)S(1)}, u32[]{:S(2)}) copy-start(f32[16,40,128]{2,1,0:T(8,128)S(1)} %all_to_all.25) | copy-start | bytes 983044
  68.7 12.2 %collective-permute-start.2 = (f32[640,128]{1,0:T(8,128)S(1)}, f32[640,128]{1,0:T(8,128)S(1)}, u32[]{:S(2)}, u32[]{:S(2)}) collective-permute-start(f32[640,128]{1,0:T(8,128)S(1)} %bitcast.10), channel_id=1, source_target_pairs={{0,1},{1,0},{2,3},{3,2},{4,5},{5,4},{6,7},{7,6},{8,9},{9,8},{10,11... | collective-permute-start | bytes 983048 | tf_op jit(solution)/shard_map/ppermute | solution.py:288
  75.7 34.8 %all-to-all-start.2 = ((f32[16,64,512]{2,1,0:T(8,128)}), f32[16,64,512]{2,1,0:T(8,128)S(1)}, u32[]{:S(2)}, u32[]{:S(2)}) async-start(f32[16,64,512]{2,1,0:T(8,128)} %bitcast.8), calls=%async_computation.2 | async-start | bytes 4194304 | tf_op jit(solution)/shard_map/all_to_all | solution.py:292
  80.9 0.7 copy-start.2
  111.5 23.0 %all-to-all-start.3 = ((f32[32,8,512]{2,1,0:T(8,128)}), f32[32,8,512]{2,1,0:T(8,128)S(1)}, u32[]{:S(2)}, u32[]{:S(2)}) async-start(f32[32,8,512]{2,1,0:T(8,128)} %bitcast.4), calls=%async_computation.3 | async-start | bytes 1048576 | tf_op jit(solution)/shard_map/all_to_all | solution.py:292
  134.5 0.8 copy-start
